TPU v7x, 256 devices: a whole 4x4x8 slice. The times are simulated.
256 devices in a mesh: blk: 32 (over y_lo, z, core), band: 8 (over y_hi, x).
Axes of the slice: x: 4, y: 4 (y_hi: 2, y_lo: 2; y = y_hi * 2 + y_lo), z: 8, core: 2. Of those that a mesh axis runs over, the one named last changes fastest.
Arguments:
- spectra: bfloat16 [256, 3, 2, 320], P('blk', None, None, 'band'), may hold values from -6 to 6
- quality: int32 [256, 3], P('blk'), may hold values 0 or 1
Outputs:
- correlations: bfloat16 [32, 256, 8, 9, 128], P(None, 'blk', 'band')
All inputs are finite; a program needn't handle non-finite values. No bound on the sum of `quality` on one device may be relied on, other than what follows from the above.
Results may differ from a plain program's by a relative error of at most 0.0012.
Values may be sent and summed in bfloat16 or wider, within the bound.
A program may use at most 64 MiB of HBM per device.

v0:
```python
import math

import jax
import jax.numpy as jnp
from jax import lax
from jax.sharding import PartitionSpec as P

F = 320
FIRST = 15
NFFT = 1500
MAXLAG = 64


def passed_along(shard, axis, by):
    peers = lax.axis_size(axis)
    return lax.ppermute(shard, axis, [(i, (i + by) % peers) for i in range(peers)])


def lag_transform(first_bin, bin_count):
    bins = jnp.arange(bin_count, dtype=jnp.int32) + first_bin + FIRST
    lag_steps = 2 * jnp.arange(2 * MAXLAG, dtype=jnp.int32) - 2 * MAXLAG + 1
    phase_index = bins[:, None] * lag_steps[None, :] % (2 * NFFT)
    phases = math.pi / NFFT * phase_index.astype(jnp.float32)
    factor = 1.0 / math.sqrt(F)
    stacked = jnp.stack([jnp.cos(phases) * factor, -jnp.sin(phases) * factor], axis=0)
    return stacked.reshape(2 * bin_count, 2 * MAXLAG)


def cross_spectra(left, right):
    left_count = left.shape[0]
    right_count = right.shape[0]
    bin_count = left.shape[3]
    left_wide = left.astype(jnp.float32)
    right_wide = right.astype(jnp.float32)
    left_real = left_wide[:, :, 0, :][:, None, :, None, :]
    left_imag = left_wide[:, :, 1, :][:, None, :, None, :]
    right_real = right_wide[:, :, 0, :][None, :, None, :, :]
    right_imag = right_wide[:, :, 1, :][None, :, None, :, :]
    real_part = left_real * right_real + left_imag * right_imag
    imag_part = left_imag * right_real - left_real * right_imag
    products = jnp.stack([real_part, imag_part], axis=4)
    return products.reshape(left_count * right_count * 9, 2 * bin_count)


def lag_block(left, right, transform):
    products = cross_spectra(left, right)
    result = jnp.dot(products, transform, precision=lax.Precision.HIGHEST)
    return result.reshape(left.shape[0], right.shape[0], 9, transform.shape[1])


def mirrored(block):
    left_count = block.shape[0]
    right_count = block.shape[1]
    lag_count = block.shape[3]
    swapped = block.reshape(left_count, right_count, 3, 3, lag_count).transpose(1, 0, 3, 2, 4)
    return swapped[..., ::-1].reshape(right_count, left_count, 9, lag_count)


def finish(own_blocks, mirror_blocks):
    received = lax.all_to_all(
        lax.all_to_all(mirror_blocks, "blk", split_axis=0, concat_axis=0, tiled=True),
        "band",
        split_axis=2,
        concat_axis=1,
        tiled=True,
    )
    return own_blocks + received


def body(spectra, quality):
    masked = spectra * quality.astype(jnp.bfloat16)[:, :, None, None]
    tile_rows = masked.shape[0]
    cycle_size = lax.axis_size("blk")
    band_size = lax.axis_size("band")
    share_rows = tile_rows // band_size
    half_cycle = cycle_size // 2
    lag_count = 2 * MAXLAG
    position = lax.axis_index("blk")
    band_place = lax.axis_index("band")
    own_blocks = jnp.zeros((cycle_size, tile_rows, share_rows, 9, lag_count), jnp.bfloat16)
    mirror_blocks = jnp.zeros((cycle_size, share_rows, tile_rows, 9, lag_count), jnp.bfloat16)

    def store(own_now, mirror_now, offset, reduced):
        rounded = reduced.astype(jnp.bfloat16)
        target = (position + offset) % cycle_size
        at_half = offset == half_cycle
        lower_half = position < half_cycle
        keep = jnp.logical_not(at_half & jnp.logical_not(lower_half))
        own_piece = jnp.where(keep, rounded, jnp.zeros_like(rounded))
        own_next = lax.dynamic_update_index_in_dim(own_now, own_piece, target, 0)
        needed = (offset >= 1) & (offset <= half_cycle - 1) | at_half & lower_half
        flipped = mirrored(rounded)
        mirror_piece = jnp.where(needed, flipped, jnp.zeros_like(flipped))
        mirror_next = lax.dynamic_update_index_in_dim(mirror_now, mirror_piece, target, 0)
        return (own_next, mirror_next)

    local_bins = masked.shape[3]
    transform = lag_transform(band_place * local_bins, local_bins)

    def reduce_block(partner):
        return lax.psum_scatter(
            lag_block(masked, partner, transform), "band", scatter_dimension=1, tiled=True
        )

    own_blocks, mirror_blocks = store(own_blocks, mirror_blocks, 0, reduce_block(masked))

    def advance(offset, carried):
        partner, own_now, mirror_now = carried
        partner = passed_along(partner, "blk", -1)
        own_now, mirror_now = store(own_now, mirror_now, offset, reduce_block(partner))
        return (partner, own_now, mirror_now)

    ignored, own_blocks, mirror_blocks = lax.fori_loop(
        1, half_cycle + 1, advance, (masked, own_blocks, mirror_blocks)
    )
    return finish(own_blocks, mirror_blocks)


def solution(mesh):
    placed = (P("blk", None, None, "band"), P("blk", None))
    return jax.shard_map(
        body,
        mesh=mesh,
        in_specs=placed,
        out_specs=P(None, "blk", "band", None, None),
        check_vma=False,
    )
```

profile of v0, /device:TPU:1, one launch (start us, length us, event | category | flops | bytes accessed | tf_op | source)
XLA Modules:
  0.0 1375.2 jit_solution(12680744321564463837)
XLA Ops:
  10.3 75.3 %reduce-scatter.9.cloned.1.call-done = f32[8,1,9,128]{3,0,2,1:T(8,128)} async-done(((f32[8,8,9,128]{3,0,2,1:T(8,128)}), f32[8,1,9,128]{3,0,2,1:T(8,128)}) %reduce-scatter.9.cloned.1.call-update) | async-done | bytes 36880
  86.3 1239.2 %while.19 = (s32[]{:T(128)}, bf16[8,3,2,40]{3,0,1,2:T(8,128)(2,1)S(1)}, bf16[32,8,1,9,128]{4,1,3,2,0:T(8,128)(2,1)S(1)}, bf16[32,1,8,9,128]{4,2,3,1,0:T(8,128)(2...) while((s32[]{:T(128)}, ...), condition=%wide.region_3.4_spmd, body=%wide.region_1.3_spmd.sunk | while | flops 70994704 | bytes 2750891 | solution.py:113
  86.4 2.6 collective-permute-start
  94.3 68.8 %reduce-scatter.11.cloned.1.call-done = f32[8,1,9,128]{3,0,2,1:T(8,128)} async-done(((f32[8,8,9,128]{3,0,2,1:T(8,128)}), f32[8,1,9,128]{3,0,2,1:T(8,128)}) %reduce-scatter.11.cloned.1.call-update) | async-done | bytes 36880 | tf_op jit(solution)/shard_map/while
  164.1 2.6 collective-permute-start
  171.9 68.8 %reduce-scatter.11.cloned.1.call-done = f32[8,1,9,128]{3,0,2,1:T(8,128)} async-done(((f32[8,8,9,128]{3,0,2,1:T(8,128)}), f32[8,1,9,128]{3,0,2,1:T(8,128)}) %reduce-scatter.11.cloned.1.call-update) | async-done | bytes 36880 | tf_op jit(solution)/shard_map/while
  241.7 2.6 collective-permute-start
  249.6 68.5 %reduce-scatter.11.cloned.1.call-done = f32[8,1,9,128]{3,0,2,1:T(8,128)} async-done(((f32[8,8,9,128]{3,0,2,1:T(8,128)}), f32[8,1,9,128]{3,0,2,1:T(8,128)}) %reduce-scatter.11.cloned.1.call-update) | async-done | bytes 36880 | tf_op jit(solution)/shard_map/while
  319.0 2.7 collective-permute-start
  326.9 68.5 %reduce-scatter.11.cloned.1.call-done = f32[8,1,9,128]{3,0,2,1:T(8,128)} async-done(((f32[8,8,9,128]{3,0,2,1:T(8,128)}), f32[8,1,9,128]{3,0,2,1:T(8,128)}) %reduce-scatter.11.cloned.1.call-update) | async-done | bytes 36880 | tf_op jit(solution)/shard_map/while
  396.4 2.6 collective-permute-start
  404.2 68.5 %reduce-scatter.11.cloned.1.call-done = f32[8,1,9,128]{3,0,2,1:T(8,128)} async-done(((f32[8,8,9,128]{3,0,2,1:T(8,128)}), f32[8,1,9,128]{3,0,2,1:T(8,128)}) %reduce-scatter.11.cloned.1.call-update) | async-done | bytes 36880 | tf_op jit(solution)/shard_map/while
  481.5 68.8 %reduce-scatter.11.cloned.1.call-done = f32[8,1,9,128]{3,0,2,1:T(8,128)} async-done(((f32[8,8,9,128]{3,0,2,1:T(8,128)}), f32[8,1,9,128]{3,0,2,1:T(8,128)}) %reduce-scatter.11.cloned.1.call-update) | async-done | bytes 36880 | tf_op jit(solution)/shard_map/while
  551.2 2.6 collective-permute-start
  559.1 68.8 %reduce-scatter.11.cloned.1.call-done = f32[8,1,9,128]{3,0,2,1:T(8,128)} async-done(((f32[8,8,9,128]{3,0,2,1:T(8,128)}), f32[8,1,9,128]{3,0,2,1:T(8,128)}) %reduce-scatter.11.cloned.1.call-update) | async-done | bytes 36880 | tf_op jit(solution)/shard_map/while
  628.9 2.6 collective-permute-start
  636.7 68.8 %reduce-scatter.11.cloned.1.call-done = f32[8,1,9,128]{3,0,2,1:T(8,128)} async-done(((f32[8,8,9,128]{3,0,2,1:T(8,128)}), f32[8,1,9,128]{3,0,2,1:T(8,128)}) %reduce-scatter.11.cloned.1.call-update) | async-done | bytes 36880 | tf_op jit(solution)/shard_map/while
  714.3 68.5 %reduce-scatter.11.cloned.1.call-done = f32[8,1,9,128]{3,0,2,1:T(8,128)} async-done(((f32[8,8,9,128]{3,0,2,1:T(8,128)}), f32[8,1,9,128]{3,0,2,1:T(8,128)}) %reduce-scatter.11.cloned.1.call-update) | async-done | bytes 36880 | tf_op jit(solution)/shard_map/while
  783.8 2.7 collective-permute-start
  791.6 68.7 %reduce-scatter.11.cloned.1.call-done = f32[8,1,9,128]{3,0,2,1:T(8,128)} async-done(((f32[8,8,9,128]{3,0,2,1:T(8,128)}), f32[8,1,9,128]{3,0,2,1:T(8,128)}) %reduce-scatter.11.cloned.1.call-update) | async-done | bytes 36880 | tf_op jit(solution)/shard_map/while
  861.3 2.7 collective-permute-start
  869.2 68.5 %reduce-scatter.11.cloned.1.call-done = f32[8,1,9,128]{3,0,2,1:T(8,128)} async-done(((f32[8,8,9,128]{3,0,2,1:T(8,128)}), f32[8,1,9,128]{3,0,2,1:T(8,128)}) %reduce-scatter.11.cloned.1.call-update) | async-done | bytes 36880 | tf_op jit(solution)/shard_map/while
  946.5 68.8 %reduce-scatter.11.cloned.1.call-done = f32[8,1,9,128]{3,0,2,1:T(8,128)} async-done(((f32[8,8,9,128]{3,0,2,1:T(8,128)}), f32[8,1,9,128]{3,0,2,1:T(8,128)}) %reduce-scatter.11.cloned.1.call-update) | async-done | bytes 36880 | tf_op jit(solution)/shard_map/while
  1024.1 68.5 %reduce-scatter.11.cloned.1.call-done = f32[8,1,9,128]{3,0,2,1:T(8,128)} async-done(((f32[8,8,9,128]{3,0,2,1:T(8,128)}), f32[8,1,9,128]{3,0,2,1:T(8,128)}) %reduce-scatter.11.cloned.1.call-update) | async-done | bytes 36880 | tf_op jit(solution)/shard_map/while
  1093.6 2.6 collective-permute-start
  1101.4 68.5 %reduce-scatter.11.cloned.1.call-done = f32[8,1,9,128]{3,0,2,1:T(8,128)} async-done(((f32[8,8,9,128]{3,0,2,1:T(8,128)}), f32[8,1,9,128]{3,0,2,1:T(8,128)}) %reduce-scatter.11.cloned.1.call-update) | async-done | bytes 36880 | tf_op jit(solution)/shard_map/while
  1170.9 2.6 collective-permute-start
  1178.7 68.5 %reduce-scatter.11.cloned.1.call-done = f32[8,1,9,128]{3,0,2,1:T(8,128)} async-done(((f32[8,8,9,128]{3,0,2,1:T(8,128)}), f32[8,1,9,128]{3,0,2,1:T(8,128)}) %reduce-scatter.11.cloned.1.call-update) | async-done | bytes 36880 | tf_op jit(solution)/shard_map/while
  1248.2 2.6 collective-permute-start
  1256.1 68.5 %reduce-scatter.11.cloned.1.call-done = f32[8,1,9,128]{3,0,2,1:T(8,128)} async-done(((f32[8,8,9,128]{3,0,2,1:T(8,128)}), f32[8,1,9,128]{3,0,2,1:T(8,128)}) %reduce-scatter.11.cloned.1.call-update) | async-done | bytes 36880 | tf_op jit(solution)/shard_map/while
  1325.5 27.6 %all_to_all.17 = bf16[32,1,8,9,128]{4,2,3,1,0:T(8,128)(2,1)S(1)} all-to-all(bf16[32,1,8,9,128]{4,2,3,1,0:T(8,128)(2,1)S(1)} %get-tuple-element.195), channel_id=1, replica_groups=mesh['blk'=32,'band'=8] {'blk'}, dimensions={0} | all-to-all | bytes 1179648 | tf_op jit(solution)/shard_map/all_to_all | solution.py:61
  1353.2 14.3 %all_to_all.18 = bf16[32,1,8,9,128]{4,0,3,1,2:T(8,128)(2,1)S(1)} all-to-all(bf16[32,1,8,9,128]{4,0,3,1,2:T(8,128)(2,1)S(1)} %copy.39), channel_id=1, replica_groups=mesh['blk'=32,'band'=8] {'band'}, dimensions={2} | all-to-all | bytes 1179648 | tf_op jit(solution)/shard_map/all_to_all | solution.py:60
  (303 shorter events, 113.2 us)
Async XLA Ops:
  6.5 79.0 %reduce-scatter.9.cloned.1.call-start = ((), (), s32[]{:S(2)}) async-start(), calls=%async_computation.4 | async-start | bytes 331776
  86.3 76.7 %reduce-scatter.11.cloned.1.call-start = ((), (), s32[]{:S(2)}) async-start(), calls=%async_computation.5 | async-start | bytes 331776 | tf_op jit(solution)/shard_map/while
  86.4 5.2 collective-permute-start
  164.0 76.7 %reduce-scatter.11.cloned.1.call-start = ((), (), s32[]{:S(2)}) async-start(), calls=%async_computation.5 | async-start | bytes 331776 | tf_op jit(solution)/shard_map/while
  164.1 5.2 collective-permute-start
  241.7 76.4 %reduce-scatter.11.cloned.1.call-start = ((), (), s32[]{:S(2)}) async-start(), calls=%async_computation.5 | async-start | bytes 331776 | tf_op jit(solution)/shard_map/while
  241.7 5.2 collective-permute-start
  319.0 76.4 %reduce-scatter.11.cloned.1.call-start = ((), (), s32[]{:S(2)}) async-start(), calls=%async_computation.5 | async-start | bytes 331776 | tf_op jit(solution)/shard_map/while
  319.0 5.2 collective-permute-start
  396.3 76.4 %reduce-scatter.11.cloned.1.call-start = ((), (), s32[]{:S(2)}) async-start(), calls=%async_computation.5 | async-start | bytes 331776 | tf_op jit(solution)/shard_map/while
  396.4 5.2 collective-permute-start
  473.6 76.7 %reduce-scatter.11.cloned.1.call-start = ((), (), s32[]{:S(2)}) async-start(), calls=%async_computation.5 | async-start | bytes 331776 | tf_op jit(solution)/shard_map/while
  473.6 5.2 collective-permute-start
  551.2 76.7 %reduce-scatter.11.cloned.1.call-start = ((), (), s32[]{:S(2)}) async-start(), calls=%async_computation.5 | async-start | bytes 331776 | tf_op jit(solution)/shard_map/while
  551.2 5.2 collective-permute-start
  628.8 76.7 %reduce-scatter.11.cloned.1.call-start = ((), (), s32[]{:S(2)}) async-start(), calls=%async_computation.5 | async-start | bytes 331776 | tf_op jit(solution)/shard_map/while
  628.9 5.2 collective-permute-start
  706.4 76.4 %reduce-scatter.11.cloned.1.call-start = ((), (), s32[]{:S(2)}) async-start(), calls=%async_computation.5 | async-start | bytes 331776 | tf_op jit(solution)/shard_map/while
  706.5 5.2 collective-permute-start
  783.7 76.6 %reduce-scatter.11.cloned.1.call-start = ((), (), s32[]{:S(2)}) async-start(), calls=%async_computation.5 | async-start | bytes 331776 | tf_op jit(solution)/shard_map/while
  783.8 5.2 collective-permute-start
  861.3 76.4 %reduce-scatter.11.cloned.1.call-start = ((), (), s32[]{:S(2)}) async-start(), calls=%async_computation.5 | async-start | bytes 331776 | tf_op jit(solution)/shard_map/while
  861.3 5.2 collective-permute-start
  938.6 76.7 %reduce-scatter.11.cloned.1.call-start = ((), (), s32[]{:S(2)}) async-start(), calls=%async_computation.5 | async-start | bytes 331776 | tf_op jit(solution)/shard_map/while
  938.7 5.2 collective-permute-start
  1016.2 76.4 %reduce-scatter.11.cloned.1.call-start = ((), (), s32[]{:S(2)}) async-start(), calls=%async_computation.5 | async-start | bytes 331776 | tf_op jit(solution)/shard_map/while
  1016.3 5.2 collective-permute-start
  1093.5 76.3 %reduce-scatter.11.cloned.1.call-start = ((), (), s32[]{:S(2)}) async-start(), calls=%async_computation.5 | async-start | bytes 331776 | tf_op jit(solution)/shard_map/while
  1093.6 5.2 collective-permute-start
  1170.8 76.4 %reduce-scatter.11.cloned.1.call-start = ((), (), s32[]{:S(2)}) async-start(), calls=%async_computation.5 | async-start | bytes 331776 | tf_op jit(solution)/shard_map/while
  1170.9 5.2 collective-permute-start
  1248.2 76.4 %reduce-scatter.11.cloned.1.call-start = ((), (), s32[]{:S(2)}) async-start(), calls=%async_computation.5 | async-start | bytes 331776 | tf_op jit(solution)/shard_map/while
  (3 other events, 6.6 us)
Sparse Core Ops, SparseCore 0:
  11.2 74.2 reduce-scatter.8
  94.3 68.7 reduce-scatter.10
  172.0 68.7 reduce-scatter.10
  249.6 68.3 reduce-scatter.10
  327.0 68.3 reduce-scatter.10
  404.3 68.3 reduce-scatter.10
  481.5 68.6 reduce-scatter.10
  559.1 68.6 reduce-scatter.10
  636.8 68.6 reduce-scatter.10
  714.4 68.3 reduce-scatter.10
  791.7 68.6 reduce-scatter.10
  869.3 68.3 reduce-scatter.10
  946.6 68.6 reduce-scatter.10
  1024.2 68.3 reduce-scatter.10
  1101.5 68.3 reduce-scatter.10
  1178.8 68.4 reduce-scatter.10
  1256.1 68.4 reduce-scatter.10
where the time goes:
time: 1380 us
  waiting for transfers between devices  1210 us (88%)
  starting transfers between devices  42.9 us (3%)
  blocking collectives  41.9 us (3%)
  other arithmetic  33.3 us (2%)
  matrix products  18.6 us (1%)
    while x32, waiting for transfers between devices  1100 us
    unnamed x2, waiting for transfers between devices  75.3 us
    ppermute x16, starting transfers between devices, passed_along(): lax.ppermute(shard, axis, [(i, (i + by) % peers) for i in range(peers)])  42.2 us
    ppermute x16, waiting for transfers between devices, passed_along(): lax.ppermute(shard, axis, [(i, (i + by) % peers) for i in range(peers)])  40.2 us
  transfers between devices with their start and end apart: 33, of which 33 were waited for; matrix products, arithmetic and copies ran while one was open for 0% of the time, Pallas kernels for 0%

commit v1 on v0

v1 whole, which is shorter than its diff:
```python
import math

import jax
import jax.numpy as jnp
import numpy as np
from jax import lax
from jax.experimental import pallas as pl
from jax.experimental.pallas import tpu as pltpu
from jax.sharding import PartitionSpec as P

F = 320
FIRST = 15
NFFT = 1500
MAXLAG = 64
LAGS = 128
COMPS = 3
TILE = 8
N_BLK = 32
N_BAND = 8
BINS = F // N_BAND
HALF = 64
CHUNKS = F // HALF
DEPTH = 2 * F
LANES = 128
RING = 8
GROUP = 8
ROWS = GROUP * COMPS * COMPS * TILE
MESH = pl.DeviceIdType.MESH


def lag_table():
    bins = np.arange(F) + FIRST
    steps = 2 * np.arange(LAGS) - 2 * MAXLAG + 1
    index = bins[:, None] * steps[None, :] % (2 * NFFT)
    phase = (np.float32(math.pi / NFFT) * index.astype(np.float32)).astype(np.float64)
    factor = 1.0 / math.sqrt(F)
    both = np.stack([np.cos(phase) * factor, np.sin(phase) * factor])
    both = both.reshape(2, CHUNKS, HALF, LAGS).transpose(1, 0, 2, 3).reshape(DEPTH, LAGS)
    high = both.astype(jnp.bfloat16)
    low = (both - high.astype(np.float64)).astype(jnp.bfloat16)
    wide = np.concatenate([high, low], axis=1)
    return np.concatenate([wide, wide], axis=0)


def ring_offset(k):
    return (k + 1) // 2 if k % 2 else (RING - k // 2) % RING


def segments():
    found = []
    for p in range(N_BAND):
        at = 0
        while at < BINS:
            chunk, lane = divmod(p * BINS + at, HALF)
            length = min(BINS - at, HALF - lane)
            found.append((p, at, length, chunk, lane))
            at += length
    return found


def kernel(
    spec_hbm, qual_hbm, table_hbm, out_ref,
    spec_v, qual_v, table_v, pieces, tile_rows, left_same, left_cross, stations, wide_rows, products,
    load_sem, first_send, first_recv, second_send, second_recv,
):
    me = lax.axis_index("blk")
    band = lax.axis_index("band")
    my_y = me // (2 * RING)
    my_z = (me // 2) % RING
    my_core = me % 2

    def peer(k, other):
        flip_y, flip_core = divmod(other, 2)
        y = (my_y + flip_y) % 2
        z = (my_z + ring_offset(k)) % RING
        core = (my_core + flip_core) % 2
        return (y * RING + z) * 2 + core

    barrier = pltpu.get_barrier_semaphore()
    for step in range(1, N_BAND):
        pl.semaphore_signal(barrier, inc=1, device_id=(me, (band + step) % N_BAND), device_id_type=MESH)
    for step in range(1, N_BLK):
        pl.semaphore_signal(barrier, inc=1, device_id=((me + step) % N_BLK, band), device_id_type=MESH)
    loads = [
        pltpu.make_async_copy(spec_hbm, spec_v, load_sem.at[0]),
        pltpu.make_async_copy(qual_hbm, qual_v, load_sem.at[1]),
        pltpu.make_async_copy(table_hbm, table_v, load_sem.at[2]),
    ]
    for load in loads:
        load.start()
    loads[0].wait()
    loads[1].wait()

    quality = qual_v[...].astype(jnp.float32)
    row = lax.broadcasted_iota(jnp.int32, (TILE, TILE), 0)
    col = lax.broadcasted_iota(jnp.int32, (TILE, TILE), 1)
    raw = spec_v[...].astype(jnp.float32)
    parts = []
    for c in range(2):
        masked = []
        for a in range(COMPS):
            usable = jnp.sum(jnp.where(row == col, quality[a : a + 1, :], 0.0), axis=1, keepdims=True)
            masked.append(raw[:, a, c, :] * usable)
        masked.append(jnp.zeros((TILE, LANES - COMPS * BINS), jnp.float32))
        parts.append(jnp.concatenate(masked, axis=1))
    pieces[band] = jnp.concatenate(parts, axis=0).astype(jnp.bfloat16)

    pl.semaphore_wait(barrier, N_BAND + N_BLK - 2)

    def first(step):
        to = (band + step) % N_BAND
        return pltpu.make_async_remote_copy(
            src_ref=pieces.at[band], dst_ref=pieces.at[band],
            send_sem=first_send.at[to], recv_sem=first_recv.at[band],
            device_id=(me, to), device_id_type=MESH,
        )

    def first_arrival(step):
        at = (band + step) % N_BAND
        return pltpu.make_async_remote_copy(
            src_ref=pieces.at[at], dst_ref=pieces.at[at],
            send_sem=first_send.at[at], recv_sem=first_recv.at[at],
            device_id=(me, at), device_id_type=MESH,
        )

    for step in (6, 2, 5, 7, 3, 1, 4):
        first(step).start()
    for step in range(1, N_BAND):
        first_arrival(step).wait_recv()

    lane = lax.broadcasted_iota(jnp.int32, (TILE, LANES), 1)
    whole = [[None] * CHUNKS for _ in range(COMPS)]
    for p, at, length, chunk, start in segments():
        piece = pieces[p].astype(jnp.float32)
        for a in range(COMPS):
            for c in range(2):
                target = HALF * c + start
                moved = pltpu.roll(piece[TILE * c : TILE * (c + 1)], (target - BINS * a - at) % LANES, 1)
                if whole[a][chunk] is None:
                    whole[a][chunk] = moved
                else:
                    here = (lane >= target) & (lane < target + length)
                    whole[a][chunk] = jnp.where(here, moved, whole[a][chunk])
    for a in range(COMPS):
        for chunk in range(CHUNKS):
            tile_rows[pl.ds((a * CHUNKS + chunk) * TILE, TILE), :] = whole[a][chunk]
    tile_rows[pl.ds(COMPS * CHUNKS * TILE, TILE), :] = jnp.zeros((TILE, LANES), jnp.float32)
    stations[me] = tile_rows[pl.ds(band, 16, stride=TILE), :].astype(jnp.bfloat16)

    def second(k, other):
        to = peer(k, other)
        return pltpu.make_async_remote_copy(
            src_ref=stations.at[me], dst_ref=stations.at[me],
            send_sem=second_send.at[to], recv_sem=second_recv.at[me],
            device_id=(to, band), device_id_type=MESH,
        )

    def second_arrival(k, other):
        at = peer(k, other)
        return pltpu.make_async_remote_copy(
            src_ref=stations.at[at], dst_ref=stations.at[at],
            send_sem=second_send.at[at], recv_sem=second_recv.at[at],
            device_id=(at, band), device_id_type=MESH,
        )

    others = [(k, other) for k in range(RING) for other in range(4) if (k, other) != (0, 0)]
    for k, other in reversed(others):
        second(k, other).start()

    for a in range(COMPS):
        for chunk in range(CHUNKS):
            here = whole[a][chunk]
            turned = pltpu.roll(here, HALF, 1)
            left_same[a, chunk] = jnp.where(lane < HALF, here, turned)
            left_cross[a, chunk] = jnp.where(lane < HALF, turned, -here)
    loads[2].wait()

    for group in range(N_BLK // GROUP):
        members = [(2 * group + s // 4, s % 4) for s in range(GROUP)]
        for s, (k, other) in enumerate(members):
            if (k, other) != (0, 0):
                second_arrival(k, other).wait_recv()
            arrived = stations[peer(k, other)].astype(jnp.float32)
            wide_rows[s, 0] = arrived
            wide_rows[s, 1] = pltpu.roll(arrived, HALF, 1)
        for chunk in range(CHUNKS):
            for pair in range(GROUP // 2):
                for b in range(COMPS):
                    right = []
                    for s in (2 * pair, 2 * pair + 1):
                        at = b * CHUNKS + chunk
                        right.append((
                            jnp.broadcast_to(wide_rows[s, 0, at : at + 1, :], (TILE, LANES)),
                            jnp.broadcast_to(wide_rows[s, 1, at : at + 1, :], (TILE, LANES)),
                        ))
                    for a in range(COMPS):
                        same = left_same[a, chunk]
                        cross = left_cross[a, chunk]
                        value = jnp.concatenate([same * r + cross * t for r, t in right], axis=0)
                        high = value.astype(jnp.bfloat16)
                        low = (value - high.astype(jnp.float32)).astype(jnp.bfloat16)
                        where = pl.ds((pair * COMPS * COMPS + a * COMPS + b) * 2 * TILE, 2 * TILE)
                        products[where, chunk * LANES : (chunk + 1) * LANES] = high
                        products[where, DEPTH + chunk * LANES : DEPTH + (chunk + 1) * LANES] = low
        result = jnp.dot(products[...], table_v[...], preferred_element_type=jnp.float32)
        summed = (result[:, :LAGS] + result[:, LAGS:]).astype(jnp.bfloat16)
        for s, (k, other) in enumerate(members):
            at = peer(k, other)
            for ab in range(COMPS * COMPS):
                start = ((s // 2) * COMPS * COMPS + ab) * 2 * TILE + (s % 2) * TILE
                out_ref[at, ab] = summed[start : start + TILE]

    for step in range(1, N_BAND):
        first(step).wait_send()
    for k, other in others:
        second(k, other).wait_send()


def body(spectra, quality):
    out = pl.pallas_call(
        kernel,
        out_shape=jax.ShapeDtypeStruct((N_BLK, COMPS * COMPS, TILE, LAGS), jnp.bfloat16),
        in_specs=[pl.BlockSpec(memory_space=pl.ANY)] * 3,
        out_specs=pl.BlockSpec(memory_space=pltpu.VMEM),
        scratch_shapes=[
            pltpu.VMEM((TILE, COMPS, 2, BINS), jnp.bfloat16),
            pltpu.VMEM((COMPS, TILE), jnp.int32),
            pltpu.VMEM((2 * DEPTH, 2 * LAGS), jnp.bfloat16),
            pltpu.VMEM((N_BAND, 2 * TILE, LANES), jnp.bfloat16),
            pltpu.VMEM((16 * TILE, LANES), jnp.float32),
            pltpu.VMEM((COMPS, CHUNKS, TILE, LANES), jnp.float32),
            pltpu.VMEM((COMPS, CHUNKS, TILE, LANES), jnp.float32),
            pltpu.VMEM((N_BLK, 16, LANES), jnp.bfloat16),
            pltpu.VMEM((GROUP, 2, 16, LANES), jnp.float32),
            pltpu.VMEM((ROWS, 2 * DEPTH), jnp.bfloat16),
            pltpu.SemaphoreType.DMA((3,)),
            pltpu.SemaphoreType.DMA((N_BAND,)),
            pltpu.SemaphoreType.DMA((N_BAND,)),
            pltpu.SemaphoreType.DMA((N_BLK,)),
            pltpu.SemaphoreType.DMA((N_BLK,)),
        ],
        compiler_params=pltpu.CompilerParams(collective_id=0, has_side_effects=True),
    )(spectra, quality.T, jnp.asarray(lag_table()))
    return out.transpose(0, 2, 1, 3)[:, :, None]


def solution(mesh):
    placed = (P("blk", None, None, "band"), P("blk", None))
    return jax.shard_map(
        body,
        mesh=mesh,
        in_specs=placed,
        out_specs=P(None, "blk", "band", None, None),
        check_vma=False,
    )
```

time: 1380 us -> 29.6 us (0.02)
  waiting for transfers between devices: 1210 us -> 0 us
  starting transfers between devices: 42.9 us -> 0 us
  blocking collectives: 41.9 us -> 0 us
  other arithmetic: 33.3 us -> 0 us
  Pallas kernels: 0 us -> 27.5 us
  matrix products: 18.6 us -> 0 us
    while x32 -> x0, waiting for transfers between devices: 1100 us -> none
    unnamed x2 -> x0, waiting for transfers between devices: 75.3 us -> none
    ppermute x16 -> x0, starting transfers between devices: 42.2 us -> none  [passed_along(): lax.ppermute(shard, axis, [(i, (i + by) % peers) for i in range(peers)])]
    all_to_all x2 -> x0, blocking collectives: 41.9 us -> none  [the longest x1 27.6 us: finish(): lax.all_to_all(mirror_blocks, 'blk', split_axis=0, concat_axis=0, tiled=T...]
    ppermute x16 -> x0, waiting for transfers between devices: 40.2 us -> none  [passed_along(): lax.ppermute(shard, axis, [(i, (i + by) % peers) for i in range(peers)])]
    pallas_call x0 -> x1, Pallas kernels: none -> 27.5 us  [body(): pl.pallas_call(kernel, out_shape=jax.ShapeDtypeStruct((N_BLK, COMPS * COM...]
    dot_general x17 -> x0, matrix products: 18.6 us -> none  [lag_block(): result = jnp.dot(products, transform, precision=lax.Precision.HIGHEST)]
  transfers between devices with their start and end apart: 33 -> 0, of which waited for: 33 -> 0; matrix products, arithmetic and copies ran while one was open for 0% -> 0% of each run, Pallas kernels for 0% -> 0%
where the time goes in v1:
time: 29.6 us; the launch traced here: 29.5 us
  Pallas kernels  27.5 us (93%)
  local copies, waits for them, and re-layouts  1.92 us (6%)
    pallas_call x1, Pallas kernels, body(): pl.pallas_call(kernel, out_shape=jax.ShapeDtypeStruct((N_BLK, COMPS * COM...  27.5 us
    unnamed x1, local copies, waits for them, and re-layouts  1.92 us

profile of v1, /device:TPU:1, one launch (start us, length us, event | category | flops | bytes accessed | tf_op | source)
XLA Modules:
  0.0 29.5 jit_solution(13803364722882201003)
XLA Ops:
  0.0 27.5 %shard_map.37 = bf16[32,9,8,128]{3,2,1,0:T(8,128)(2,1)} custom-call(bf16[8,3,2,40]{3,2,1,0:T(2,128)(2,1)} %spec_hbm.1, s32[3,8]{1,0:T(4,128)} %bitcast.7, bf16[1280,256]{1,0:T(8,128)(2,1)} %constant.2.clone.table_hbm), custom_call_target="tpu_custom_call" | custom-call | tf_op jit(solution)/shard_map/pallas_call | solution.py:220
  27.5 1.9 %copy.6 = bf16[32,8,1,9,128]{4,1,3,2,0:T(8,128)(2,1)} copy(bf16[32,8,1,9,128]{4,1,3,2,0:T(8,128)(2,1)} %bitcast.6) | data formatting | bytes 1179648

commit v2 on v1

--- a/solution.py
+++ b/solution.py
@@ -42,8 +42,11 @@
     return np.concatenate([wide, wide], axis=0)
 
 
-def ring_offset(k):
-    return (k + 1) // 2 if k % 2 else (RING - k // 2) % RING
+RING_ORDER = (0, 1, 2, 3, 7, 6, 5, 4)
+
+
+def index_at(place):
+    return ((place // 2) % 2 * RING + place // 4) * 2 + place % 2
 
 
 def segments():
@@ -61,26 +64,30 @@
 def kernel(
     spec_hbm, qual_hbm, table_hbm, out_ref,
     spec_v, qual_v, table_v, pieces, tile_rows, left_same, left_cross, stations, wide_rows, products,
-    load_sem, first_send, first_recv, second_send, second_recv,
+    entered, load_sem, first_send, first_recv, second_send, second_recv,
 ):
     me = lax.axis_index("blk")
     band = lax.axis_index("band")
     my_y = me // (2 * RING)
     my_z = (me // 2) % RING
     my_core = me % 2
+    my_place = my_z * 4 + my_y * 2 + my_core
 
     def peer(k, other):
         flip_y, flip_core = divmod(other, 2)
         y = (my_y + flip_y) % 2
-        z = (my_z + ring_offset(k)) % RING
+        z = (my_z + RING_ORDER[k]) % RING
         core = (my_core + flip_core) % 2
         return (y * RING + z) * 2 + core
 
     barrier = pltpu.get_barrier_semaphore()
     for step in range(1, N_BAND):
         pl.semaphore_signal(barrier, inc=1, device_id=(me, (band + step) % N_BAND), device_id_type=MESH)
-    for step in range(1, N_BLK):
-        pl.semaphore_signal(barrier, inc=1, device_id=((me + step) % N_BLK, band), device_id_type=MESH)
+
+    @pl.loop(my_place + 1, N_BLK)
+    def _(place):
+        pl.semaphore_signal(barrier, inc=1, device_id=(index_at(place), band), device_id_type=MESH)
+
     loads = [
         pltpu.make_async_copy(spec_hbm, spec_v, load_sem.at[0]),
         pltpu.make_async_copy(qual_hbm, qual_v, load_sem.at[1]),
@@ -105,7 +112,7 @@
         parts.append(jnp.concatenate(masked, axis=1))
     pieces[band] = jnp.concatenate(parts, axis=0).astype(jnp.bfloat16)
 
-    pl.semaphore_wait(barrier, N_BAND + N_BLK - 2)
+    pl.semaphore_wait(barrier, N_BAND - 1 + my_place)
 
     def first(step):
         to = (band + step) % N_BAND
@@ -125,6 +132,11 @@
 
     for step in (6, 2, 5, 7, 3, 1, 4):
         first(step).start()
+
+    @pl.loop(0, my_place)
+    def _(place):
+        pl.semaphore_signal(entered.at[me], inc=1, device_id=(index_at(place), band), device_id_type=MESH)
+
     for step in range(1, N_BAND):
         first_arrival(step).wait_recv()
 
@@ -147,25 +159,21 @@
     tile_rows[pl.ds(COMPS * CHUNKS * TILE, TILE), :] = jnp.zeros((TILE, LANES), jnp.float32)
     stations[me] = tile_rows[pl.ds(band, 16, stride=TILE), :].astype(jnp.bfloat16)
 
-    def second(k, other):
-        to = peer(k, other)
+    def second(at, to):
         return pltpu.make_async_remote_copy(
-            src_ref=stations.at[me], dst_ref=stations.at[me],
-            send_sem=second_send.at[to], recv_sem=second_recv.at[me],
+            src_ref=stations.at[at], dst_ref=stations.at[at],
+            send_sem=second_send.at[to], recv_sem=second_recv.at[at],
             device_id=(to, band), device_id_type=MESH,
         )
 
-    def second_arrival(k, other):
-        at = peer(k, other)
-        return pltpu.make_async_remote_copy(
-            src_ref=stations.at[at], dst_ref=stations.at[at],
-            send_sem=second_send.at[at], recv_sem=second_recv.at[at],
-            device_id=(at, band), device_id_type=MESH,
-        )
-
-    others = [(k, other) for k in range(RING) for other in range(4) if (k, other) != (0, 0)]
-    for k, other in reversed(others):
-        second(k, other).start()
+    @pl.loop(0, my_place)
+    def _(place):
+        second(me, index_at(place)).start()
+
+    @pl.loop(my_place + 1, N_BLK)
+    def _(place):
+        pl.semaphore_wait(entered.at[index_at(place)], 1)
+        second(me, index_at(place)).start()
 
     for a in range(COMPS):
         for chunk in range(CHUNKS):
@@ -179,7 +187,7 @@
         members = [(2 * group + s // 4, s % 4) for s in range(GROUP)]
         for s, (k, other) in enumerate(members):
             if (k, other) != (0, 0):
-                second_arrival(k, other).wait_recv()
+                second(peer(k, other), me).wait_recv()
             arrived = stations[peer(k, other)].astype(jnp.float32)
             wide_rows[s, 0] = arrived
             wide_rows[s, 1] = pltpu.roll(arrived, HALF, 1)
@@ -212,14 +220,16 @@
 
     for step in range(1, N_BAND):
         first(step).wait_send()
-    for k, other in others:
-        second(k, other).wait_send()
+
+    @pl.loop(1, N_BLK)
+    def _(step):
+        second(me, (me + step) % N_BLK).wait_send()
 
 
 def body(spectra, quality):
     out = pl.pallas_call(
         kernel,
-        out_shape=jax.ShapeDtypeStruct((N_BLK, COMPS * COMPS, TILE, LAGS), jnp.bfloat16),
+        out_shape=pltpu.VMEM((N_BLK, COMPS * COMPS, TILE, LAGS), jnp.bfloat16),
         in_specs=[pl.BlockSpec(memory_space=pl.ANY)] * 3,
         out_specs=pl.BlockSpec(memory_space=pltpu.VMEM),
         scratch_shapes=[
@@ -233,6 +243,7 @@
             pltpu.VMEM((N_BLK, 16, LANES), jnp.bfloat16),
             pltpu.VMEM((GROUP, 2, 16, LANES), jnp.float32),
             pltpu.VMEM((ROWS, 2 * DEPTH), jnp.bfloat16),
+            pltpu.SemaphoreType.REGULAR((N_BLK,)),
             pltpu.SemaphoreType.DMA((3,)),
             pltpu.SemaphoreType.DMA((N_BAND,)),
             pltpu.SemaphoreType.DMA((N_BAND,)),

time: 29.6 us -> 24.6 us (0.83)
  Pallas kernels: 27.5 us -> 23.6 us
  local copies, waits for them, and re-layouts: 1.92 us -> 0.82 us
    pallas_call x1, Pallas kernels: 27.5 us -> 23.6 us  [body(): pl.pallas_call(kernel, out_shape=pltpu.VMEM((N_BLK, COMPS * COMPS, TILE,...]
    unnamed x1, local copies, waits for them, and re-layouts: 1.92 us -> 0.82 us
where the time goes in v2:
time: 24.6 us; the launch traced here: 24.5 us
  Pallas kernels  23.6 us (96%)
  local copies, waits for them, and re-layouts  0.82 us (3%)
    pallas_call x1, Pallas kernels, body(): pl.pallas_call(kernel, out_shape=pltpu.VMEM((N_BLK, COMPS * COMPS, TILE,...  23.6 us
    unnamed x1, local copies, waits for them, and re-layouts  0.82 us

profile of v2, /device:TPU:1, one launch (start us, length us, event | category | flops | bytes accessed | tf_op | source)
XLA Modules:
  0.0 24.5 jit_solution(13837615270293636711)
XLA Ops:
  0.0 23.6 %shard_map.37 = bf16[32,9,8,128]{3,2,1,0:T(8,128)(2,1)S(1)} custom-call(bf16[8,3,2,40]{3,2,1,0:T(2,128)(2,1)} %spec_hbm.1, s32[3,8]{1,0:T(4,128)} %bitcast.7, bf16[1280,256]{1,0:T(8,128)(2,1)} %constant.2.clone.table_hbm), custom_call_target="tpu_custom_call" | custom-call | tf_op jit(solution)/shard_map/pallas_call | solution.py:230
  23.6 0.8 %copy.6 = bf16[32,8,1,9,128]{4,1,3,2,0:T(8,128)(2,1)} copy(bf16[32,8,1,9,128]{4,1,3,2,0:T(8,128)(2,1)S(1)} %bitcast.6) | data formatting | bytes 1179648

commit v3 on v2

--- a/solution.py
+++ b/solution.py
@@ -43,6 +43,8 @@
 
 
 RING_ORDER = (0, 1, 2, 3, 7, 6, 5, 4)
+HUB = 30
+HUB_ORDER = sorted((place for place in range(N_BLK) if place != HUB), key=lambda place: -min((place // 4 - HUB // 4) % RING, (HUB // 4 - place // 4) % RING))
 
 
 def index_at(place):
@@ -64,29 +66,21 @@
 def kernel(
     spec_hbm, qual_hbm, table_hbm, out_ref,
     spec_v, qual_v, table_v, pieces, tile_rows, left_same, left_cross, stations, wide_rows, products,
-    entered, load_sem, first_send, first_recv, second_send, second_recv,
+    all_in, load_sem, first_send, first_recv, second_send, second_recv,
 ):
     me = lax.axis_index("blk")
     band = lax.axis_index("band")
-    my_y = me // (2 * RING)
-    my_z = (me // 2) % RING
-    my_core = me % 2
+    my_y = lax.div(me, 2 * RING)
+    my_z = lax.rem(lax.div(me, 2), RING)
+    my_core = lax.rem(me, 2)
     my_place = my_z * 4 + my_y * 2 + my_core
 
     def peer(k, other):
         flip_y, flip_core = divmod(other, 2)
-        y = (my_y + flip_y) % 2
-        z = (my_z + RING_ORDER[k]) % RING
-        core = (my_core + flip_core) % 2
+        y = lax.rem(my_y + flip_y, 2)
+        z = lax.rem(my_z + RING_ORDER[k], RING)
+        core = lax.rem(my_core + flip_core, 2)
         return (y * RING + z) * 2 + core
-
-    barrier = pltpu.get_barrier_semaphore()
-    for step in range(1, N_BAND):
-        pl.semaphore_signal(barrier, inc=1, device_id=(me, (band + step) % N_BAND), device_id_type=MESH)
-
-    @pl.loop(my_place + 1, N_BLK)
-    def _(place):
-        pl.semaphore_signal(barrier, inc=1, device_id=(index_at(place), band), device_id_type=MESH)
 
     loads = [
         pltpu.make_async_copy(spec_hbm, spec_v, load_sem.at[0]),
@@ -95,6 +89,16 @@
     ]
     for load in loads:
         load.start()
+
+    barrier = pltpu.get_barrier_semaphore()
+
+    @pl.when(my_place != HUB)
+    def _():
+        pl.semaphore_signal(barrier, inc=1, device_id=(index_at(HUB), band), device_id_type=MESH)
+
+    for step in range(1, N_BAND):
+        pl.semaphore_signal(barrier, inc=1, device_id=(me, lax.rem(band + step, N_BAND)), device_id_type=MESH)
+
     loads[0].wait()
     loads[1].wait()
 
@@ -112,33 +116,30 @@
         parts.append(jnp.concatenate(masked, axis=1))
     pieces[band] = jnp.concatenate(parts, axis=0).astype(jnp.bfloat16)
 
-    pl.semaphore_wait(barrier, N_BAND - 1 + my_place)
+    pl.semaphore_wait(barrier, jnp.where(my_place == HUB, N_BAND + N_BLK - 2, N_BAND - 1))
+
+    @pl.when(my_place == HUB)
+    def _():
+        for place in HUB_ORDER:
+            pl.semaphore_signal(all_in, inc=1, device_id=(index_at(place), band), device_id_type=MESH)
 
     def first(step):
-        to = (band + step) % N_BAND
+        to = lax.rem(band + step, N_BAND)
         return pltpu.make_async_remote_copy(
             src_ref=pieces.at[band], dst_ref=pieces.at[band],
-            send_sem=first_send.at[to], recv_sem=first_recv.at[band],
+            send_sem=first_send, recv_sem=first_recv,
             device_id=(me, to), device_id_type=MESH,
         )
 
-    def first_arrival(step):
-        at = (band + step) % N_BAND
-        return pltpu.make_async_remote_copy(
-            src_ref=pieces.at[at], dst_ref=pieces.at[at],
-            send_sem=first_send.at[at], recv_sem=first_recv.at[at],
-            device_id=(me, at), device_id_type=MESH,
-        )
-
     for step in (6, 2, 5, 7, 3, 1, 4):
         first(step).start()
 
-    @pl.loop(0, my_place)
-    def _(place):
-        pl.semaphore_signal(entered.at[me], inc=1, device_id=(index_at(place), band), device_id_type=MESH)
-
-    for step in range(1, N_BAND):
-        first_arrival(step).wait_recv()
+    all_first = pltpu.make_async_remote_copy(
+        src_ref=pieces.at[pl.ds(0, N_BAND - 1)], dst_ref=pieces.at[pl.ds(0, N_BAND - 1)],
+        send_sem=first_send, recv_sem=first_recv,
+        device_id=(me, lax.rem(band + 1, N_BAND)), device_id_type=MESH,
+    )
+    all_first.wait_recv()
 
     lane = lax.broadcasted_iota(jnp.int32, (TILE, LANES), 1)
     whole = [[None] * CHUNKS for _ in range(COMPS)]
@@ -159,21 +160,28 @@
     tile_rows[pl.ds(COMPS * CHUNKS * TILE, TILE), :] = jnp.zeros((TILE, LANES), jnp.float32)
     stations[me] = tile_rows[pl.ds(band, 16, stride=TILE), :].astype(jnp.bfloat16)
 
-    def second(at, to):
+    def second(to):
         return pltpu.make_async_remote_copy(
-            src_ref=stations.at[at], dst_ref=stations.at[at],
-            send_sem=second_send.at[to], recv_sem=second_recv.at[at],
+            src_ref=stations.at[me], dst_ref=stations.at[me],
+            send_sem=second_send, recv_sem=second_recv.at[my_z],
             device_id=(to, band), device_id_type=MESH,
         )
 
-    @pl.loop(0, my_place)
-    def _(place):
-        second(me, index_at(place)).start()
-
-    @pl.loop(my_place + 1, N_BLK)
-    def _(place):
-        pl.semaphore_wait(entered.at[index_at(place)], 1)
-        second(me, index_at(place)).start()
+    def second_bytes(count, z):
+        return pltpu.make_async_remote_copy(
+            src_ref=stations.at[pl.ds(0, count)], dst_ref=stations.at[pl.ds(0, count)],
+            send_sem=second_send, recv_sem=second_recv.at[z],
+            device_id=(lax.rem(me + 1, N_BLK), band), device_id_type=MESH,
+        )
+
+    @pl.when(my_place != HUB)
+    def _():
+        pl.semaphore_wait(all_in, 1)
+
+    for place in range(N_BLK):
+        @pl.when(my_place != place)
+        def _():
+            second(index_at(place)).start()
 
     for a in range(COMPS):
         for chunk in range(CHUNKS):
@@ -185,9 +193,9 @@
 
     for group in range(N_BLK // GROUP):
         members = [(2 * group + s // 4, s % 4) for s in range(GROUP)]
+        for k in (2 * group, 2 * group + 1):
+            second_bytes(4 if k else 3, lax.rem(my_z + RING_ORDER[k], RING)).wait_recv()
         for s, (k, other) in enumerate(members):
-            if (k, other) != (0, 0):
-                second(peer(k, other), me).wait_recv()
             arrived = stations[peer(k, other)].astype(jnp.float32)
             wide_rows[s, 0] = arrived
             wide_rows[s, 1] = pltpu.roll(arrived, HALF, 1)
@@ -218,12 +226,8 @@
                 start = ((s // 2) * COMPS * COMPS + ab) * 2 * TILE + (s % 2) * TILE
                 out_ref[at, ab] = summed[start : start + TILE]
 
-    for step in range(1, N_BAND):
-        first(step).wait_send()
-
-    @pl.loop(1, N_BLK)
-    def _(step):
-        second(me, (me + step) % N_BLK).wait_send()
+    all_first.wait_send()
+    second_bytes(N_BLK - 1, my_z).wait_send()
 
 
 def body(spectra, quality):
@@ -243,12 +247,12 @@
             pltpu.VMEM((N_BLK, 16, LANES), jnp.bfloat16),
             pltpu.VMEM((GROUP, 2, 16, LANES), jnp.float32),
             pltpu.VMEM((ROWS, 2 * DEPTH), jnp.bfloat16),
-            pltpu.SemaphoreType.REGULAR((N_BLK,)),
+            pltpu.SemaphoreType.REGULAR,
             pltpu.SemaphoreType.DMA((3,)),
-            pltpu.SemaphoreType.DMA((N_BAND,)),
-            pltpu.SemaphoreType.DMA((N_BAND,)),
-            pltpu.SemaphoreType.DMA((N_BLK,)),
-            pltpu.SemaphoreType.DMA((N_BLK,)),
+            pltpu.SemaphoreType.DMA,
+            pltpu.SemaphoreType.DMA,
+            pltpu.SemaphoreType.DMA,
+            pltpu.SemaphoreType.DMA((RING,)),
         ],
         compiler_params=pltpu.CompilerParams(collective_id=0, has_side_effects=True),
     )(spectra, quality.T, jnp.asarray(lag_table()))

time: 24.6 us -> 22.5 us (0.915)
  Pallas kernels: 23.6 us -> 21.6 us
    pallas_call x1, Pallas kernels: 23.6 us -> 21.6 us  [body(): pl.pallas_call(kernel, out_shape=pltpu.VMEM((N_BLK, COMPS * COMPS, TILE,...]
where the time goes in v3:
time: 22.5 us; the launch traced here: 22.4 us
  Pallas kernels  21.6 us (96%)
  local copies, waits for them, and re-layouts  0.82 us (4%)
    pallas_call x1, Pallas kernels, body(): pl.pallas_call(kernel, out_shape=pltpu.VMEM((N_BLK, COMPS * COMPS, TILE,...  21.6 us
    unnamed x1, local copies, waits for them, and re-layouts  0.82 us

profile of v3, /device:TPU:1, one launch (start us, length us, event | category | flops | bytes accessed | tf_op | source)
XLA Modules:
  0.0 22.4 jit_solution(1279294060520851516)
XLA Ops:
  0.0 21.6 %shard_map.37 = bf16[32,9,8,128]{3,2,1,0:T(8,128)(2,1)S(1)} custom-call(bf16[8,3,2,40]{3,2,1,0:T(2,128)(2,1)} %spec_hbm.1, s32[3,8]{1,0:T(4,128)} %bitcast.7, bf16[1280,256]{1,0:T(8,128)(2,1)} %constant.2.clone.table_hbm), custom_call_target="tpu_custom_call" | custom-call | tf_op jit(solution)/shard_map/pallas_call | solution.py:234
  21.6 0.8 %copy.6 = bf16[32,8,1,9,128]{4,1,3,2,0:T(8,128)(2,1)} copy(bf16[32,8,1,9,128]{4,1,3,2,0:T(8,128)(2,1)S(1)} %bitcast.6) | data formatting | bytes 1179648

commit v4 on v3

--- a/solution.py
+++ b/solution.py
@@ -24,7 +24,9 @@
 LANES = 128
 RING = 8
 GROUP = 8
-ROWS = GROUP * COMPS * COMPS * TILE
+WIDE = 2 * LANES
+STEPS = 3
+UNITS = 2
 MESH = pl.DeviceIdType.MESH
 
 
@@ -39,7 +41,7 @@
     high = both.astype(jnp.bfloat16)
     low = (both - high.astype(np.float64)).astype(jnp.bfloat16)
     wide = np.concatenate([high, low], axis=1)
-    return np.concatenate([wide, wide], axis=0)
+    return np.concatenate([wide, wide[-LANES:]], axis=0)
 
 
 RING_ORDER = (0, 1, 2, 3, 7, 6, 5, 4)
@@ -65,7 +67,7 @@
 
 def kernel(
     spec_hbm, qual_hbm, table_hbm, out_ref,
-    spec_v, qual_v, table_v, pieces, tile_rows, left_same, left_cross, stations, wide_rows, products,
+    spec_v, qual_v, table_v, pieces, tile_rows, left_same, left_cross, stations, wide_rows,
     all_in, load_sem, first_send, first_recv, second_send, second_recv,
 ):
     me = lax.axis_index("blk")
@@ -191,41 +193,57 @@
             left_cross[a, chunk] = jnp.where(lane < HALF, turned, -here)
     loads[2].wait()
 
-    for group in range(N_BLK // GROUP):
-        members = [(2 * group + s // 4, s % 4) for s in range(GROUP)]
-        for k in (2 * group, 2 * group + 1):
-            second_bytes(4 if k else 3, lax.rem(my_z + RING_ORDER[k], RING)).wait_recv()
-        for s, (k, other) in enumerate(members):
-            arrived = stations[peer(k, other)].astype(jnp.float32)
-            wide_rows[s, 0] = arrived
-            wide_rows[s, 1] = pltpu.roll(arrived, HALF, 1)
-        for chunk in range(CHUNKS):
+    def split_cross(pair, a, b, chunk):
+        rows = []
+        at = b * CHUNKS + chunk
+        for s in (2 * pair, 2 * pair + 1):
+            straight = jnp.broadcast_to(wide_rows[s, 0, at : at + 1, :], (TILE, LANES))
+            turned = jnp.broadcast_to(wide_rows[s, 1, at : at + 1, :], (TILE, LANES))
+            rows.append(left_same[a, chunk] * straight + left_cross[a, chunk] * turned)
+        value = jnp.concatenate(rows, axis=0)
+        high = value.astype(jnp.bfloat16)
+        return high, (value - high.astype(jnp.float32)).astype(jnp.bfloat16)
+
+    def correlate(*totals):
+        for group in range(N_BLK // GROUP):
+            members = [(2 * group + s // 4, s % 4) for s in range(GROUP)]
+            for k in (2 * group, 2 * group + 1):
+                second_bytes(4 if k else 3, lax.rem(my_z + RING_ORDER[k], RING)).wait_recv()
+            for s, (k, other) in enumerate(members):
+                arrived = stations[peer(k, other)].astype(jnp.float32)
+                wide_rows[s, 0] = arrived
+                wide_rows[s, 1] = pltpu.roll(arrived, HALF, 1)
+            for step in range(STEPS):
+                register = (group * STEPS + step) % 2
+                weights = table_v[pl.ds(step * WIDE, WIDE), :]
+                for unit in range(UNITS):
+                    pltpu.matmul_push_rhs(weights, staging_register=register, mxu_index=unit)
+                fresh = [True] * UNITS
+                for pair in range(GROUP // 2):
+                    unit = pair % UNITS
+                    for b in range(COMPS):
+                        for a in range(COMPS):
+                            parts = [split_cross(pair, a, b, chunk) for chunk in range(2 * step, min(2 * step + 2, CHUNKS))]
+                            sums = totals[pair * COMPS * COMPS + a * COMPS + b]
+                            if len(parts) == 1:
+                                operands = [jnp.concatenate(parts[0], axis=1)]
+                            else:
+                                operands = [jnp.concatenate([part[i] for part in parts], axis=1) for i in range(2)]
+                            for operand in operands:
+                                pltpu.matmul_acc_lhs(sums, operand, load_staged_rhs=register if fresh[unit] else None)
+                                fresh[unit] = False
             for pair in range(GROUP // 2):
-                for b in range(COMPS):
-                    right = []
-                    for s in (2 * pair, 2 * pair + 1):
-                        at = b * CHUNKS + chunk
-                        right.append((
-                            jnp.broadcast_to(wide_rows[s, 0, at : at + 1, :], (TILE, LANES)),
-                            jnp.broadcast_to(wide_rows[s, 1, at : at + 1, :], (TILE, LANES)),
-                        ))
-                    for a in range(COMPS):
-                        same = left_same[a, chunk]
-                        cross = left_cross[a, chunk]
-                        value = jnp.concatenate([same * r + cross * t for r, t in right], axis=0)
-                        high = value.astype(jnp.bfloat16)
-                        low = (value - high.astype(jnp.float32)).astype(jnp.bfloat16)
-                        where = pl.ds((pair * COMPS * COMPS + a * COMPS + b) * 2 * TILE, 2 * TILE)
-                        products[where, chunk * LANES : (chunk + 1) * LANES] = high
-                        products[where, DEPTH + chunk * LANES : DEPTH + (chunk + 1) * LANES] = low
-        result = jnp.dot(products[...], table_v[...], preferred_element_type=jnp.float32)
-        summed = (result[:, :LAGS] + result[:, LAGS:]).astype(jnp.bfloat16)
-        for s, (k, other) in enumerate(members):
-            at = peer(k, other)
-            for ab in range(COMPS * COMPS):
-                start = ((s // 2) * COMPS * COMPS + ab) * 2 * TILE + (s % 2) * TILE
-                out_ref[at, ab] = summed[start : start + TILE]
-
+                for ab in range(COMPS * COMPS):
+                    both = pltpu.matmul_pop(totals[pair * COMPS * COMPS + ab])
+                    summed = both[:, :LAGS] + both[:, LAGS:]
+                    for half in range(2):
+                        k, other = members[2 * pair + half]
+                        out_ref[peer(k, other), ab] = summed[half * TILE : (half + 1) * TILE].astype(jnp.bfloat16)
+
+    pl.run_scoped(
+        correlate,
+        *[pltpu.ACC(i // (COMPS * COMPS) % UNITS)((2 * TILE, WIDE), jnp.float32) for i in range(GROUP // 2 * COMPS * COMPS)],
+    )
     all_first.wait_send()
     second_bytes(N_BLK - 1, my_z).wait_send()
 
@@ -239,14 +257,13 @@
         scratch_shapes=[
             pltpu.VMEM((TILE, COMPS, 2, BINS), jnp.bfloat16),
             pltpu.VMEM((COMPS, TILE), jnp.int32),
-            pltpu.VMEM((2 * DEPTH, 2 * LAGS), jnp.bfloat16),
+            pltpu.VMEM((DEPTH + LANES, 2 * LAGS), jnp.bfloat16),
             pltpu.VMEM((N_BAND, 2 * TILE, LANES), jnp.bfloat16),
             pltpu.VMEM((16 * TILE, LANES), jnp.float32),
             pltpu.VMEM((COMPS, CHUNKS, TILE, LANES), jnp.float32),
             pltpu.VMEM((COMPS, CHUNKS, TILE, LANES), jnp.float32),
             pltpu.VMEM((N_BLK, 16, LANES), jnp.bfloat16),
             pltpu.VMEM((GROUP, 2, 16, LANES), jnp.float32),
-            pltpu.VMEM((ROWS, 2 * DEPTH), jnp.bfloat16),
             pltpu.SemaphoreType.REGULAR,
             pltpu.SemaphoreType.DMA((3,)),
             pltpu.SemaphoreType.DMA,

time: 22.5 us -> 21.5 us (0.956)
  Pallas kernels: 21.6 us -> 20.5 us
    pallas_call x1, Pallas kernels: 21.6 us -> 20.5 us  [body(): pl.pallas_call(kernel, out_shape=pltpu.VMEM((N_BLK, COMPS * COMPS, TILE,...]
where the time goes in v4:
time: 21.5 us; the launch traced here: 21.3 us
  Pallas kernels  20.5 us (95%)
  local copies, waits for them, and re-layouts  0.82 us (4%)
    pallas_call x1, Pallas kernels, body(): pl.pallas_call(kernel, out_shape=pltpu.VMEM((N_BLK, COMPS * COMPS, TILE,...  20.5 us
    unnamed x1, local copies, waits for them, and re-layouts  0.82 us

profile of v4, /device:TPU:1, one launch (start us, length us, event | category | flops | bytes accessed | tf_op | source)
XLA Modules:
  0.0 21.3 jit_solution(17358873498473585861)
XLA Ops:
  0.0 20.5 %shard_map.37 = bf16[32,9,8,128]{3,2,1,0:T(8,128)(2,1)S(1)} custom-call(bf16[8,3,2,40]{3,2,1,0:T(2,128)(2,1)} %spec_hbm.1, s32[3,8]{1,0:T(4,128)} %bitcast.7, bf16[768,256]{1,0:T(8,128)(2,1)} %constant.2.clone.table_hbm), custom_call_target="tpu_custom_call" | custom-call | tf_op jit(solution)/shard_map/pallas_call | solution.py:252
  20.5 0.8 %copy.6 = bf16[32,8,1,9,128]{4,1,3,2,0:T(8,128)(2,1)} copy(bf16[32,8,1,9,128]{4,1,3,2,0:T(8,128)(2,1)S(1)} %bitcast.6) | data formatting | bytes 1179648

commit v5 on v4

--- a/solution.py
+++ b/solution.py
@@ -45,8 +45,8 @@
 
 
 RING_ORDER = (0, 1, 2, 3, 7, 6, 5, 4)
-HUB = 30
-HUB_ORDER = sorted((place for place in range(N_BLK) if place != HUB), key=lambda place: -min((place // 4 - HUB // 4) % RING, (HUB // 4 - place // 4) % RING))
+HUB_Z = (3, 5, 6, 6, 6, 7, 7, 7)
+HUB_ORDER = [4 * z + other for z in (4, 3, 5, 2, 6, 1, 7, 0) for other in range(4)]
 
 
 def index_at(place):
@@ -67,8 +67,8 @@
 
 def kernel(
     spec_hbm, qual_hbm, table_hbm, out_ref,
-    spec_v, qual_v, table_v, pieces, tile_rows, left_same, left_cross, stations, wide_rows,
-    all_in, load_sem, first_send, first_recv, second_send, second_recv,
+    spec_v, qual_v, table_v, pieces, rows_out, rows_in, left_same, left_cross, stations, wide_rows,
+    all_in, load_sem, first_send, first_recv, second_send, second_recv, third_send, third_recv,
 ):
     me = lax.axis_index("blk")
     band = lax.axis_index("band")
@@ -92,11 +92,15 @@
     for load in loads:
         load.start()
 
+    hub_z = HUB_Z[-1]
+    for b in range(N_BAND - 1):
+        hub_z = jnp.where(band == b, HUB_Z[b], hub_z)
+    hub = 4 * hub_z + 2
     barrier = pltpu.get_barrier_semaphore()
 
-    @pl.when(my_place != HUB)
+    @pl.when(my_place != hub)
     def _():
-        pl.semaphore_signal(barrier, inc=1, device_id=(index_at(HUB), band), device_id_type=MESH)
+        pl.semaphore_signal(barrier, inc=1, device_id=(index_at(hub), band), device_id_type=MESH)
 
     for step in range(1, N_BAND):
         pl.semaphore_signal(barrier, inc=1, device_id=(me, lax.rem(band + step, N_BAND)), device_id_type=MESH)
@@ -117,50 +121,77 @@
         masked.append(jnp.zeros((TILE, LANES - COMPS * BINS), jnp.float32))
         parts.append(jnp.concatenate(masked, axis=1))
     pieces[band] = jnp.concatenate(parts, axis=0).astype(jnp.bfloat16)
-
-    pl.semaphore_wait(barrier, jnp.where(my_place == HUB, N_BAND + N_BLK - 2, N_BAND - 1))
-
-    @pl.when(my_place == HUB)
+    flat = jnp.concatenate(parts, axis=1)
+    for station in range(TILE):
+        rows_out[station] = flat[station : station + 1, :]
+    rows_in[band] = rows_out[band]
+
+    pl.semaphore_wait(barrier, jnp.where(my_place == hub, N_BAND + N_BLK - 2, N_BAND - 1))
+
+    @pl.when(my_place == hub)
     def _():
         for place in HUB_ORDER:
-            pl.semaphore_signal(all_in, inc=1, device_id=(index_at(place), band), device_id_type=MESH)
+            @pl.when(my_place != place)
+            def _():
+                pl.semaphore_signal(all_in, inc=1, device_id=(index_at(place), band), device_id_type=MESH)
 
     def first(step):
         to = lax.rem(band + step, N_BAND)
         return pltpu.make_async_remote_copy(
-            src_ref=pieces.at[band], dst_ref=pieces.at[band],
+            src_ref=rows_out.at[to], dst_ref=rows_in.at[band],
             send_sem=first_send, recv_sem=first_recv,
             device_id=(me, to), device_id_type=MESH,
         )
 
+    def third(step):
+        to = lax.rem(band + step, N_BAND)
+        return pltpu.make_async_remote_copy(
+            src_ref=pieces.at[band], dst_ref=pieces.at[band],
+            send_sem=third_send, recv_sem=third_recv,
+            device_id=(me, to), device_id_type=MESH,
+        )
+
+    def whole_bytes(ref, send_sem, recv_sem):
+        return pltpu.make_async_remote_copy(
+            src_ref=ref.at[pl.ds(0, N_BAND - 1)], dst_ref=ref.at[pl.ds(0, N_BAND - 1)],
+            send_sem=send_sem, recv_sem=recv_sem,
+            device_id=(me, lax.rem(band + 1, N_BAND)), device_id_type=MESH,
+        )
+
     for step in (6, 2, 5, 7, 3, 1, 4):
         first(step).start()
-
-    all_first = pltpu.make_async_remote_copy(
-        src_ref=pieces.at[pl.ds(0, N_BAND - 1)], dst_ref=pieces.at[pl.ds(0, N_BAND - 1)],
-        send_sem=first_send, recv_sem=first_recv,
-        device_id=(me, lax.rem(band + 1, N_BAND)), device_id_type=MESH,
-    )
+    all_first = whole_bytes(rows_in, first_send, first_recv)
+    all_third = whole_bytes(pieces, third_send, third_recv)
+
+    lane = lax.broadcasted_iota(jnp.int32, (TILE, LANES), 1)
+
+    def assemble(piece):
+        whole = [[None] * CHUNKS for _ in range(COMPS)]
+        for p, at, length, chunk, start in segments():
+            for c in range(2):
+                values = piece(p, c)
+                for a in range(COMPS):
+                    target = HALF * c + start
+                    moved = pltpu.roll(values, (target - BINS * a - at) % LANES, 1)
+                    if whole[a][chunk] is None:
+                        whole[a][chunk] = moved
+                    else:
+                        here = (lane >= target) & (lane < target + length)
+                        whole[a][chunk] = jnp.where(here, moved, whole[a][chunk])
+        return whole
+
     all_first.wait_recv()
-
-    lane = lax.broadcasted_iota(jnp.int32, (TILE, LANES), 1)
-    whole = [[None] * CHUNKS for _ in range(COMPS)]
-    for p, at, length, chunk, start in segments():
-        piece = pieces[p].astype(jnp.float32)
-        for a in range(COMPS):
-            for c in range(2):
-                target = HALF * c + start
-                moved = pltpu.roll(piece[TILE * c : TILE * (c + 1)], (target - BINS * a - at) % LANES, 1)
-                if whole[a][chunk] is None:
-                    whole[a][chunk] = moved
-                else:
-                    here = (lane >= target) & (lane < target + length)
-                    whole[a][chunk] = jnp.where(here, moved, whole[a][chunk])
-    for a in range(COMPS):
-        for chunk in range(CHUNKS):
-            tile_rows[pl.ds((a * CHUNKS + chunk) * TILE, TILE), :] = whole[a][chunk]
-    tile_rows[pl.ds(COMPS * CHUNKS * TILE, TILE), :] = jnp.zeros((TILE, LANES), jnp.float32)
-    stations[me] = tile_rows[pl.ds(band, 16, stride=TILE), :].astype(jnp.bfloat16)
+    mine = assemble(lambda p, c: jnp.broadcast_to(rows_in[p, :, c * LANES : (c + 1) * LANES], (TILE, LANES)))
+    sublane = lax.broadcasted_iota(jnp.int32, (TILE, LANES), 0)
+    halves = []
+    for half in range(2):
+        rows = jnp.zeros((TILE, LANES), jnp.float32)
+        for r in range(TILE):
+            if half * TILE + r < COMPS * CHUNKS:
+                a, chunk = divmod(half * TILE + r, CHUNKS)
+                rows = jnp.where(sublane == r, mine[a][chunk], rows)
+        halves.append(rows)
+    stations[me] = jnp.concatenate(halves, axis=0).astype(jnp.bfloat16)
 
     def second(to):
         return pltpu.make_async_remote_copy(
@@ -176,7 +207,7 @@
             device_id=(lax.rem(me + 1, N_BLK), band), device_id_type=MESH,
         )
 
-    @pl.when(my_place != HUB)
+    @pl.when(my_place != hub)
     def _():
         pl.semaphore_wait(all_in, 1)
 
@@ -184,6 +215,11 @@
         @pl.when(my_place != place)
         def _():
             second(index_at(place)).start()
+
+    for step in (6, 2, 5, 7, 3, 1, 4):
+        third(step).start()
+    all_third.wait_recv()
+    whole = assemble(lambda p, c: pieces[p, c * TILE : (c + 1) * TILE, :].astype(jnp.float32))
 
     for a in range(COMPS):
         for chunk in range(CHUNKS):
@@ -206,8 +242,8 @@
 
     def correlate(*totals):
         for group in range(N_BLK // GROUP):
-            members = [(2 * group + s // 4, s % 4) for s in range(GROUP)]
-            for k in (2 * group, 2 * group + 1):
+            members = [divmod(group * GROUP + s, 4) for s in range(GROUP)]
+            for k in sorted({k for k, _ in members}):
                 second_bytes(4 if k else 3, lax.rem(my_z + RING_ORDER[k], RING)).wait_recv()
             for s, (k, other) in enumerate(members):
                 arrived = stations[peer(k, other)].astype(jnp.float32)
@@ -245,6 +281,7 @@
         *[pltpu.ACC(i // (COMPS * COMPS) % UNITS)((2 * TILE, WIDE), jnp.float32) for i in range(GROUP // 2 * COMPS * COMPS)],
     )
     all_first.wait_send()
+    all_third.wait_send()
     second_bytes(N_BLK - 1, my_z).wait_send()
 
 
@@ -259,7 +296,8 @@
             pltpu.VMEM((COMPS, TILE), jnp.int32),
             pltpu.VMEM((DEPTH + LANES, 2 * LAGS), jnp.bfloat16),
             pltpu.VMEM((N_BAND, 2 * TILE, LANES), jnp.bfloat16),
-            pltpu.VMEM((16 * TILE, LANES), jnp.float32),
+            pltpu.VMEM((N_BAND, 1, 2 * LANES), jnp.float32),
+            pltpu.VMEM((N_BAND, 1, 2 * LANES), jnp.float32),
             pltpu.VMEM((COMPS, CHUNKS, TILE, LANES), jnp.float32),
             pltpu.VMEM((COMPS, CHUNKS, TILE, LANES), jnp.float32),
             pltpu.VMEM((N_BLK, 16, LANES), jnp.bfloat16),
@@ -270,6 +308,8 @@
             pltpu.SemaphoreType.DMA,
             pltpu.SemaphoreType.DMA,
             pltpu.SemaphoreType.DMA((RING,)),
+            pltpu.SemaphoreType.DMA,
+            pltpu.SemaphoreType.DMA,
         ],
         compiler_params=pltpu.CompilerParams(collective_id=0, has_side_effects=True),
     )(spectra, quality.T, jnp.asarray(lag_table()))

time: 21.5 us -> 21 us (0.977)
  Pallas kernels: 20.5 us -> 20.1 us
    pallas_call x1, Pallas kernels: 20.5 us -> 20.1 us  [body(): pl.pallas_call(kernel, out_shape=pltpu.VMEM((N_BLK, COMPS * COMPS, TILE,...]
where the time goes in v5:
time: 21 us; the launch traced here: 20.9 us
  Pallas kernels  20.1 us (96%)
  local copies, waits for them, and re-layouts  0.82 us (4%)
    pallas_call x1, Pallas kernels, body(): pl.pallas_call(kernel, out_shape=pltpu.VMEM((N_BLK, COMPS * COMPS, TILE,...  20.1 us
    unnamed x1, local copies, waits for them, and re-layouts  0.82 us

profile of v5, /device:TPU:1, one launch (start us, length us, event | category | flops | bytes accessed | tf_op | source)
XLA Modules:
  0.0 20.9 jit_solution(1671306392222959584)
XLA Ops:
  0.0 20.1 %shard_map.37 = bf16[32,9,8,128]{3,2,1,0:T(8,128)(2,1)S(1)} custom-call(bf16[8,3,2,40]{3,2,1,0:T(2,128)(2,1)} %spec_hbm.1, s32[3,8]{1,0:T(4,128)} %bitcast.7, bf16[768,256]{1,0:T(8,128)(2,1)} %constant.2.clone.table_hbm), custom_call_target="tpu_custom_call" | custom-call | tf_op jit(solution)/shard_map/pallas_call | solution.py:289
  20.1 0.8 %copy.6 = bf16[32,8,1,9,128]{4,1,3,2,0:T(8,128)(2,1)} copy(bf16[32,8,1,9,128]{4,1,3,2,0:T(8,128)(2,1)S(1)} %bitcast.6) | data formatting | bytes 1179648

commit v6 on v5

--- a/solution.py
+++ b/solution.py
@@ -160,6 +160,8 @@
 
     for step in (6, 2, 5, 7, 3, 1, 4):
         first(step).start()
+    for step in (6, 2, 5, 7, 3, 1, 4):
+        third(step).start()
     all_first = whole_bytes(rows_in, first_send, first_recv)
     all_third = whole_bytes(pieces, third_send, third_recv)
 
@@ -211,13 +213,11 @@
     def _():
         pl.semaphore_wait(all_in, 1)
 
-    for place in range(N_BLK):
+    for place in [1, 3, 0, 2] + list(range(4, N_BLK)):
         @pl.when(my_place != place)
         def _():
             second(index_at(place)).start()
 
-    for step in (6, 2, 5, 7, 3, 1, 4):
-        third(step).start()
     all_third.wait_recv()
     whole = assemble(lambda p, c: pieces[p, c * TILE : (c + 1) * TILE, :].astype(jnp.float32))
 

time: 21 us -> 20.9 us (level)
  no operation moved by 1% of the time
where the time goes in v6:
time: 20.9 us; the launch traced here: 20.7 us
  Pallas kernels  19.9 us (95%)
  local copies, waits for them, and re-layouts  0.82 us (4%)
    pallas_call x1, Pallas kernels, body(): pl.pallas_call(kernel, out_shape=pltpu.VMEM((N_BLK, COMPS * COMPS, TILE,...  19.9 us
    unnamed x1, local copies, waits for them, and re-layouts  0.82 us

profile of v6, /device:TPU:1, one launch (start us, length us, event | category | flops | bytes accessed | tf_op | source)
XLA Modules:
  0.0 20.7 jit_solution(5317344096070946648)
XLA Ops:
  0.0 19.9 %shard_map.37 = bf16[32,9,8,128]{3,2,1,0:T(8,128)(2,1)S(1)} custom-call(bf16[8,3,2,40]{3,2,1,0:T(2,128)(2,1)} %spec_hbm.1, s32[3,8]{1,0:T(4,128)} %bitcast.7, bf16[768,256]{1,0:T(8,128)(2,1)} %constant.2.clone.table_hbm), custom_call_target="tpu_custom_call" | custom-call | tf_op jit(solution)/shard_map/pallas_call | solution.py:289
  19.9 0.8 %copy.6 = bf16[32,8,1,9,128]{4,1,3,2,0:T(8,128)(2,1)} copy(bf16[32,8,1,9,128]{4,1,3,2,0:T(8,128)(2,1)S(1)} %bitcast.6) | data formatting | bytes 1179648

commit v7 on v6

--- a/solution.py
+++ b/solution.py
@@ -89,8 +89,8 @@
         pltpu.make_async_copy(qual_hbm, qual_v, load_sem.at[1]),
         pltpu.make_async_copy(table_hbm, table_v, load_sem.at[2]),
     ]
-    for load in loads:
-        load.start()
+    loads[0].start()
+    loads[1].start()
 
     hub_z = HUB_Z[-1]
     for b in range(N_BAND - 1):
@@ -102,7 +102,7 @@
     def _():
         pl.semaphore_signal(barrier, inc=1, device_id=(index_at(hub), band), device_id_type=MESH)
 
-    for step in range(1, N_BAND):
+    for step in (6, 2, 5, 7, 3, 1, 4):
         pl.semaphore_signal(barrier, inc=1, device_id=(me, lax.rem(band + step, N_BAND)), device_id_type=MESH)
 
     loads[0].wait()
@@ -162,6 +162,7 @@
         first(step).start()
     for step in (6, 2, 5, 7, 3, 1, 4):
         third(step).start()
+    loads[2].start()
     all_first = whole_bytes(rows_in, first_send, first_recv)
     all_third = whole_bytes(pieces, third_send, third_recv)
 

time: 20.9 us -> 20.9 us (level)
  no operation moved by 1% of the time
where the time goes in v7:
time: 20.9 us; the launch traced here: 20.8 us
  Pallas kernels  19.9 us (95%)
  local copies, waits for them, and re-layouts  0.82 us (4%)
    pallas_call x1, Pallas kernels, body(): pl.pallas_call(kernel, out_shape=pltpu.VMEM((N_BLK, COMPS * COMPS, TILE,...  19.9 us
    unnamed x1, local copies, waits for them, and re-layouts  0.82 us

profile of v7, /device:TPU:1, one launch (start us, length us, event | category | flops | bytes accessed | tf_op | source)
XLA Modules:
  0.0 20.8 jit_solution(14589844847048766710)
XLA Ops:
  0.0 19.9 %shard_map.37 = bf16[32,9,8,128]{3,2,1,0:T(8,128)(2,1)S(1)} custom-call(bf16[8,3,2,40]{3,2,1,0:T(2,128)(2,1)} %spec_hbm.1, s32[3,8]{1,0:T(4,128)} %bitcast.7, bf16[768,256]{1,0:T(8,128)(2,1)} %constant.2.clone.table_hbm), custom_call_target="tpu_custom_call" | custom-call | tf_op jit(solution)/shard_map/pallas_call | solution.py:290
  19.9 0.8 %copy.6 = bf16[32,8,1,9,128]{4,1,3,2,0:T(8,128)(2,1)} copy(bf16[32,8,1,9,128]{4,1,3,2,0:T(8,128)(2,1)S(1)} %bitcast.6) | data formatting | bytes 1179648

commit v8 on v6

--- a/solution.py
+++ b/solution.py
@@ -213,7 +213,7 @@
     def _():
         pl.semaphore_wait(all_in, 1)
 
-    for place in [1, 3, 0, 2] + list(range(4, N_BLK)):
+    for place in [4 * z + other for z in range(RING) for other in (1, 3, 0, 2)]:
         @pl.when(my_place != place)
         def _():
             second(index_at(place)).start()

time: 20.9 us -> 20.9 us (level)
  no operation moved by 1% of the time
where the time goes in v8:
time: 20.9 us; the launch traced here: 20.7 us
  Pallas kernels  19.9 us (95%)
  local copies, waits for them, and re-layouts  0.82 us (4%)
    pallas_call x1, Pallas kernels, body(): pl.pallas_call(kernel, out_shape=pltpu.VMEM((N_BLK, COMPS * COMPS, TILE,...  19.9 us
    unnamed x1, local copies, waits for them, and re-layouts  0.82 us

profile of v8, /device:TPU:1, one launch (start us, length us, event | category | flops | bytes accessed | tf_op | source)
XLA Modules:
  0.0 20.7 jit_solution(15083068126558395447)
XLA Ops:
  0.0 19.9 %shard_map.37 = bf16[32,9,8,128]{3,2,1,0:T(8,128)(2,1)S(1)} custom-call(bf16[8,3,2,40]{3,2,1,0:T(2,128)(2,1)} %spec_hbm.1, s32[3,8]{1,0:T(4,128)} %bitcast.7, bf16[768,256]{1,0:T(8,128)(2,1)} %constant.2.clone.table_hbm), custom_call_target="tpu_custom_call" | custom-call | tf_op jit(solution)/shard_map/pallas_call | solution.py:289
  19.9 0.8 %copy.6 = bf16[32,8,1,9,128]{4,1,3,2,0:T(8,128)(2,1)} copy(bf16[32,8,1,9,128]{4,1,3,2,0:T(8,128)(2,1)S(1)} %bitcast.6) | data formatting | bytes 1179648
